TPU v7x, 32 devices: a whole 2x2x4 slice. The times are simulated.
32 devices in a mesh: replica: 8 (over z, y), shard: 4 (over x, core).
Axes of the slice: x: 2, y: 2, z: 4, core: 2. Of those that a mesh axis runs over, the one named last changes fastest.
Arguments:
- hidden_in: bfloat16 [4096, 1024], P(('replica', 'shard')), may hold values from -6 to 6
- out_grad: bfloat16 [4096, 1024], P(('replica', 'shard')), may hold values from -6 to 6
- lengths: int32 [32, 4], P(('replica', 'shard')), may hold values from 1 to 64, 128 in all within a row
- norm1_gain: bfloat16 [1024], P('shard'), may hold values from 0.099609375 to 1.8984375
- norm1_bias: bfloat16 [1024], P('shard'), may hold values from -3 to 3
- qkv_weight: bfloat16 [1024, 3072], P('shard'), may hold values from -0.1875 to 0.1875
- query_bias: bfloat16 [1024], P('shard'), may hold values from -3 to 3
- value_bias: bfloat16 [1024], P('shard'), may hold values from -3 to 3
- out_weight: bfloat16 [1024, 1024], P('shard'), may hold values from -0.75 to 0.75
- out_bias: bfloat16 [1024], P('shard'), may hold values from -3 to 3
- norm2_gain: bfloat16 [1024], P('shard'), may hold values from 0.099609375 to 1.8984375
- norm2_bias: bfloat16 [1024], P('shard'), may hold values from -3 to 3
- up_weight: bfloat16 [1024, 4096], P('shard'), may hold values from -0.1875 to 0.1875
- up_bias: bfloat16 [4096], P('shard'), may hold values from -3 to 3
- down_weight: bfloat16 [4096, 1024], P('shard'), may hold values from -0.125 to 0.125
- down_bias: bfloat16 [1024], P('shard'), may hold values from -3 to 3
Outputs:
- hidden_out: bfloat16 [4096, 1024], P(('replica', 'shard'))
- in_grad: bfloat16 [4096, 1024], P(('replica', 'shard'))
- norm1_gain_grad: float32 [1024], P('shard')
- norm1_bias_grad: float32 [1024], P('shard')
- qkv_weight_grad: float32 [1024, 3072], P('shard')
- query_bias_grad: float32 [1024], P('shard')
- value_bias_grad: float32 [1024], P('shard')
- out_weight_grad: float32 [1024, 1024], P('shard')
- out_bias_grad: float32 [1024], P('shard')
- norm2_gain_grad: float32 [1024], P('shard')
- norm2_bias_grad: float32 [1024], P('shard')
- up_weight_grad: float32 [1024, 4096], P('shard')
- up_bias_grad: float32 [4096], P('shard')
- down_weight_grad: float32 [4096, 1024], P('shard')
- down_bias_grad: float32 [1024], P('shard')
Inputs may be any that keep to these rules, and one draw needn't show every extreme that they name: The 4 lengths of each device add up to 128, and the largest of all is 64.
All inputs are finite; a program needn't handle non-finite values.
Results may differ from a plain program's by a relative error of at most 0.018.
Values may be sent and summed in bfloat16 or wider, within the bound.
A program may use at most 192 MiB of HBM per device.

v0:
```python
import math
import jax
import jax.numpy as jnp
from jax import lax
from jax.sharding import PartitionSpec as P

HEADS = 16
HEAD_DIM = 64
EPSILON = 1e-05
TANH_SCALE = math.sqrt(2.0 / math.pi)
CUBIC = 0.044715


def product(left, right):
    return jnp.dot(left, right, preferred_element_type=jnp.float32)


def left_product(left, right):
    return lax.dot_general(
        left, right, (((0,), (0,)), ((), ())), preferred_element_type=jnp.float32
    )


def right_product(left, right):
    return lax.dot_general(
        left, right, (((1,), (1,)), ((), ())), preferred_element_type=jnp.float32
    )


def column_term(left, right):
    return left_product(left, right)


def gelu_parts(pre_act):
    inner_arg = TANH_SCALE * (pre_act + CUBIC * pre_act * pre_act * pre_act)
    tangent = jnp.tanh(inner_arg)
    gelu_value = 0.5 * pre_act * (1.0 + tangent)
    gelu_slope = 0.5 * (1.0 + tangent) + 0.5 * pre_act * (1.0 - tangent * tangent) * TANH_SCALE * (
        1.0 + 3.0 * CUBIC * pre_act * pre_act
    )
    return (gelu_value, gelu_slope)


def layer_norm(inputs, gain_row, bias_row):
    average = jnp.mean(inputs, axis=-1, keepdims=True)
    centred = inputs - average
    inv_std = lax.rsqrt(jnp.mean(centred * centred, axis=-1, keepdims=True) + EPSILON)
    normed = centred * inv_std
    return (normed * gain_row.astype(jnp.float32) + bias_row.astype(jnp.float32), normed, inv_std)


def norm_back(upstream, normed, inv_std, gain_row):
    scaled = upstream * gain_row.astype(jnp.float32)
    first_term = jnp.mean(scaled, axis=-1, keepdims=True)
    second_term = jnp.mean(scaled * normed, axis=-1, keepdims=True)
    input_grad = inv_std * (scaled - first_term - normed * second_term)
    return (input_grad, jnp.sum(upstream * normed, axis=0), jnp.sum(upstream, axis=0))


def seq_mask(lengths, row_count):
    seq_ends = jnp.cumsum(lengths, axis=-1)
    places = jnp.arange(row_count, dtype=jnp.int32)
    segment = jnp.sum((places[None, :, None] >= seq_ends[:, None, :]).astype(jnp.int32), axis=-1)
    causal = places[None, :] <= places[:, None]
    return (segment[:, :, None] == segment[:, None, :]) & causal[None]


def split_heads(flat_rows, groups):
    return flat_rows.reshape(groups, -1, HEADS, HEAD_DIM)


def attend_forward(queries, key_rows, values, allowed):
    groups = allowed.shape[0]
    scale_factor = 1.0 / math.sqrt(HEAD_DIM)
    head_q = split_heads(queries, groups)
    head_k = split_heads(key_rows, groups)
    head_v = split_heads(values, groups)
    scores = (
        jnp.einsum("gqhd,gkhd->ghqk", head_q, head_k, preferred_element_type=jnp.float32)
        * scale_factor
    )
    visible = allowed[:, None]
    row_total = jnp.sum(jnp.where(visible, jnp.exp(scores), 0.0), axis=-1, keepdims=True)
    log_total = jnp.log(row_total)
    probs_round = jnp.where(visible, jnp.exp(scores - log_total), 0.0).astype(jnp.bfloat16)
    context = jnp.einsum("ghqk,gkhd->gqhd", probs_round, head_v, preferred_element_type=jnp.float32)
    return (context.reshape(-1, HEADS * HEAD_DIM).astype(jnp.bfloat16), log_total)


def attend_backward(queries, key_rows, values, allowed, log_total, context_grad):
    groups = allowed.shape[0]
    scale_factor = 1.0 / math.sqrt(HEAD_DIM)
    head_q = split_heads(queries, groups)
    head_k = split_heads(key_rows, groups)
    head_v = split_heads(values, groups)
    head_g = split_heads(context_grad, groups)
    scores = (
        jnp.einsum("gqhd,gkhd->ghqk", head_q, head_k, preferred_element_type=jnp.float32)
        * scale_factor
    )
    visible = allowed[:, None]
    exact_probs = jnp.where(visible, jnp.exp(scores - log_total), 0.0)
    probs_round = exact_probs.astype(jnp.bfloat16)
    prob_grad = jnp.einsum("gqhd,gkhd->ghqk", head_g, head_v, preferred_element_type=jnp.float32)
    value_grad = jnp.einsum(
        "ghqk,gqhd->gkhd", probs_round, head_g, preferred_element_type=jnp.float32
    )
    row_delta = jnp.sum(exact_probs * prob_grad, axis=-1, keepdims=True)
    score_grad = (exact_probs * (prob_grad - row_delta) * scale_factor).astype(jnp.bfloat16)
    query_grad = jnp.einsum(
        "ghqk,gkhd->gqhd", score_grad, head_k, preferred_element_type=jnp.float32
    )
    key_grad = jnp.einsum("ghqk,gqhd->gkhd", score_grad, head_q, preferred_element_type=jnp.float32)
    model_width = HEADS * HEAD_DIM
    return (
        query_grad.reshape(-1, model_width),
        key_grad.reshape(-1, model_width),
        value_grad.reshape(-1, model_width),
    )


def local(
    hidden_in,
    out_grad,
    lengths,
    norm1_gain,
    norm1_bias,
    qkv_weight,
    query_bias,
    value_bias,
    out_weight,
    out_bias,
    norm2_gain,
    norm2_bias,
    up_weight,
    up_bias,
    down_weight,
    down_bias,
):
    (
        gain_one,
        bias_one,
        qkv_full,
        qbias_full,
        vbias_full,
        outw_full,
        outb_full,
        gain_two,
        bias_two,
        upw_full,
        upb_full,
        downw_full,
        downb_full,
    ) = (
        lax.all_gather(norm1_gain, "shard", axis=0, tiled=True),
        lax.all_gather(norm1_bias, "shard", axis=0, tiled=True),
        lax.all_gather(qkv_weight, "shard", axis=0, tiled=True),
        lax.all_gather(query_bias, "shard", axis=0, tiled=True),
        lax.all_gather(value_bias, "shard", axis=0, tiled=True),
        lax.all_gather(out_weight, "shard", axis=0, tiled=True),
        lax.all_gather(out_bias, "shard", axis=0, tiled=True),
        lax.all_gather(norm2_gain, "shard", axis=0, tiled=True),
        lax.all_gather(norm2_bias, "shard", axis=0, tiled=True),
        lax.all_gather(up_weight, "shard", axis=0, tiled=True),
        lax.all_gather(up_bias, "shard", axis=0, tiled=True),
        lax.all_gather(down_weight, "shard", axis=0, tiled=True),
        lax.all_gather(down_bias, "shard", axis=0, tiled=True),
    )
    allowed = seq_mask(lengths, hidden_in.shape[0])
    model_width = hidden_in.shape[1]
    inputs_wide = hidden_in.astype(jnp.float32)
    first_out, normed_one, inv_one = layer_norm(inputs_wide, gain_one, bias_one)
    first_in = first_out.astype(jnp.bfloat16)
    projected = product(first_in, qkv_full)
    queries = (projected[:, :model_width] + qbias_full.astype(jnp.float32)).astype(jnp.bfloat16)
    key_rows = projected[:, model_width : 2 * model_width].astype(jnp.bfloat16)
    values = (projected[:, 2 * model_width :] + vbias_full.astype(jnp.float32)).astype(jnp.bfloat16)
    context, log_total = attend_forward(queries, key_rows, values, allowed)
    residual = inputs_wide + product(context, outw_full) + outb_full.astype(jnp.float32)
    second_out, normed_two, inv_two = layer_norm(residual, gain_two, bias_two)
    second_in = second_out.astype(jnp.bfloat16)
    pre_act = product(second_in, upw_full) + upb_full.astype(jnp.float32)
    activ_value, gelu_slope = gelu_parts(pre_act)
    activated = activ_value.astype(jnp.bfloat16)
    hidden_out = (
        residual + product(activated, downw_full) + downb_full.astype(jnp.float32)
    ).astype(jnp.bfloat16)
    back_qkv, back_out, back_up, back_down, back_gain1, back_gain2 = (
        qkv_full,
        outw_full,
        upw_full,
        downw_full,
        gain_one,
        gain_two,
    )
    upstream = out_grad.astype(jnp.float32)
    down_owned = lax.psum_scatter(
        column_term(activated, out_grad).astype(jnp.bfloat16),
        "shard",
        scatter_dimension=0,
        tiled=True,
    )
    down_bgrad = jnp.sum(upstream, axis=0)
    pre_grad = right_product(out_grad, back_down) * gelu_slope
    pre_round = pre_grad.astype(jnp.bfloat16)
    up_bgrad = jnp.sum(pre_grad, axis=0)
    up_owned = lax.psum_scatter(
        column_term(second_in, pre_round).astype(jnp.bfloat16),
        "shard",
        scatter_dimension=0,
        tiled=True,
    )
    second_grad = right_product(pre_round, back_up)
    norm_two_in, gain2_grad, bias2_grad = norm_back(second_grad, normed_two, inv_two, back_gain2)
    resid_grad = upstream + norm_two_in
    resid_round = resid_grad.astype(jnp.bfloat16)
    out_bgrad = jnp.sum(resid_grad, axis=0)
    out_owned = lax.psum_scatter(
        column_term(context, resid_round).astype(jnp.bfloat16),
        "shard",
        scatter_dimension=0,
        tiled=True,
    )
    context_grad = right_product(resid_round, back_out).astype(jnp.bfloat16)
    query_grad, key_grad, value_grad = attend_backward(
        queries, key_rows, values, allowed, log_total, context_grad
    )
    query_bgrad = jnp.sum(query_grad, axis=0)
    value_bgrad = jnp.sum(value_grad, axis=0)
    qkv_grad = jnp.concatenate([query_grad, key_grad, value_grad], axis=1).astype(jnp.bfloat16)
    qkv_owned = lax.psum_scatter(
        column_term(first_in, qkv_grad).astype(jnp.bfloat16),
        "shard",
        scatter_dimension=0,
        tiled=True,
    )
    first_grad = right_product(qkv_grad, back_qkv)
    norm_one_in, gain1_grad, bias1_grad = norm_back(first_grad, normed_one, inv_one, back_gain1)
    in_grad = (resid_grad + norm_one_in).astype(jnp.bfloat16)
    (
        gain1_own,
        bias1_own,
        qbias_own,
        vbias_own,
        outb_own,
        gain2_own,
        bias2_own,
        upb_own,
        downb_own,
    ) = (
        lax.psum_scatter(
            gain1_grad.astype(jnp.bfloat16), "shard", scatter_dimension=0, tiled=True
        ).astype(jnp.float32),
        lax.psum_scatter(
            bias1_grad.astype(jnp.bfloat16), "shard", scatter_dimension=0, tiled=True
        ).astype(jnp.float32),
        lax.psum_scatter(
            query_bgrad.astype(jnp.bfloat16), "shard", scatter_dimension=0, tiled=True
        ).astype(jnp.float32),
        lax.psum_scatter(
            value_bgrad.astype(jnp.bfloat16), "shard", scatter_dimension=0, tiled=True
        ).astype(jnp.float32),
        lax.psum_scatter(
            out_bgrad.astype(jnp.bfloat16), "shard", scatter_dimension=0, tiled=True
        ).astype(jnp.float32),
        lax.psum_scatter(
            gain2_grad.astype(jnp.bfloat16), "shard", scatter_dimension=0, tiled=True
        ).astype(jnp.float32),
        lax.psum_scatter(
            bias2_grad.astype(jnp.bfloat16), "shard", scatter_dimension=0, tiled=True
        ).astype(jnp.float32),
        lax.psum_scatter(
            up_bgrad.astype(jnp.bfloat16), "shard", scatter_dimension=0, tiled=True
        ).astype(jnp.float32),
        lax.psum_scatter(
            down_bgrad.astype(jnp.bfloat16), "shard", scatter_dimension=0, tiled=True
        ).astype(jnp.float32),
    )
    (
        gain1_total,
        bias1_total,
        qkv_total,
        qbias_total,
        vbias_total,
        outw_total,
        outb_total,
        gain2_total,
        bias2_total,
        upw_total,
        upb_total,
        downw_total,
        downb_total,
    ) = (
        lax.psum(gain1_own.astype(jnp.bfloat16), "replica").astype(jnp.float32),
        lax.psum(bias1_own.astype(jnp.bfloat16), "replica").astype(jnp.float32),
        lax.psum(qkv_owned, "replica").astype(jnp.float32),
        lax.psum(qbias_own.astype(jnp.bfloat16), "replica").astype(jnp.float32),
        lax.psum(vbias_own.astype(jnp.bfloat16), "replica").astype(jnp.float32),
        lax.psum(out_owned, "replica").astype(jnp.float32),
        lax.psum(outb_own.astype(jnp.bfloat16), "replica").astype(jnp.float32),
        lax.psum(gain2_own.astype(jnp.bfloat16), "replica").astype(jnp.float32),
        lax.psum(bias2_own.astype(jnp.bfloat16), "replica").astype(jnp.float32),
        lax.psum(up_owned, "replica").astype(jnp.float32),
        lax.psum(upb_own.astype(jnp.bfloat16), "replica").astype(jnp.float32),
        lax.psum(down_owned, "replica").astype(jnp.float32),
        lax.psum(downb_own.astype(jnp.bfloat16), "replica").astype(jnp.float32),
    )
    return (
        hidden_out,
        in_grad,
        gain1_total,
        bias1_total,
        qkv_total,
        qbias_total,
        vbias_total,
        outw_total,
        outb_total,
        gain2_total,
        bias2_total,
        upw_total,
        upb_total,
        downw_total,
        downb_total,
    )


def solution(mesh):
    in_specs = (
        P(("replica", "shard"), None),
        P(("replica", "shard"), None),
        P(("replica", "shard"), None),
        P("shard"),
        P("shard"),
        P("shard", None),
        P("shard"),
        P("shard"),
        P("shard", None),
        P("shard"),
        P("shard"),
        P("shard"),
        P("shard", None),
        P("shard"),
        P("shard", None),
        P("shard"),
    )
    out_specs = (
        P(("replica", "shard"), None),
        P(("replica", "shard"), None),
        P("shard"),
        P("shard"),
        P("shard", None),
        P("shard"),
        P("shard"),
        P("shard", None),
        P("shard"),
        P("shard"),
        P("shard"),
        P("shard", None),
        P("shard"),
        P("shard", None),
        P("shard"),
    )
    return jax.shard_map(local, mesh=mesh, in_specs=in_specs, out_specs=out_specs, check_vma=False)
```

profile of v0, /device:TPU:0, one launch (start us, length us, event | category | flops | bytes accessed | tf_op | source)
XLA Modules:
  0.0 687.5 jit_solution(8565300499013674690)
XLA Ops:
  10.1 6.0 all-gather.4
  16.2 5.4 all-gather.1
  21.6 5.2 all-gather
  26.8 5.2 all-gather.3
  32.0 5.2 all-gather.2
  37.3 5.4 all_gather.49
  42.6 5.2 all-gather.6
  47.9 5.2 all-gather.5
  64.3 18.7 %all-gather.15.cloned.1.call-done = bf16[1024,1024]{1,0:T(8,128)(2,1)} async-done(((bf16[256,1024]{1,0:T(8,128)(2,1)}), bf16[1024,1024]{1,0:T(8,128)(2,1)}) %all-gather.15.cloned.1.call-update) | async-done | bytes 2097168 | tf_op jit(solution)/shard_map/all_gather | solution.py:160
  85.4 57.5 %all-gather.17.cloned.1.call-done = bf16[1024,4096]{1,0:T(8,128)(2,1)} async-done(((bf16[256,4096]{1,0:T(8,128)(2,1)}), bf16[1024,4096]{1,0:T(8,128)(2,1)}) %all-gather.17.cloned.1.call-update) | async-done | bytes 8388624 | tf_op jit(solution)/shard_map/all_gather | solution.py:164
  147.6 54.9 %all-gather.19.cloned.1.call-done = bf16[4096,1024]{1,0:T(8,128)(2,1)} async-done(((bf16[1024,1024]{1,0:T(8,128)(2,1)}), bf16[4096,1024]{1,0:T(8,128)(2,1)}) %all-gather.19.cloned.1.call-update) | async-done | bytes 8388624 | tf_op jit(solution)/shard_map/all_gather | solution.py:166
  202.5 7.1 %fusion.74 = (bf16[4096]{0:T(1024)(128)(2,1)S(1)}, bf16[128,4096]{1,0:T(8,128)(2,1)S(1)}) fusion(f32[128,4096]{1,0:T(8,128)S(1)} %convolution_add_fusion, bf16[128,1024]{1,0:T(8,128)(2,1)S(1)} %copy-done.4, bf16[4096,1024]{1,0:T(8,128)(2,1)} %all-gather.19.cloned.1.call-done), kind=kOutput, calls=%fused_computation.108 | convolution fusion | flops 1084223488 | bytes 11804672 | tf_op jit(solution)/shard_map/dot_general | solution.py:25
  234.5 5.8 convolution_convert_fusion.2
  240.4 6.9 %convolution_convert_fusion.1 = bf16[1024,4096]{1,0:T(8,128)(2,1)} fusion(bf16[128,4096]{1,0:T(8,128)(2,1)} %copy-done.3, f32[128,1024]{1,0:T(8,128)S(1)} %get-tuple-element.54, f32[1024]{0:T(1024)S(1)} %bitcast.77, f32[1024]{0:T(1024)S(1)} %bitcast.69, f32[128]{0:T(128)S(1)} %add_rsqrt_fusion, f32[128]{0:T(128)S(1)} %broadcast_multiply_fusion.4), kind=kOutput, calls=%fused_computation.3 | convolution fusion | flops 1078591488 | bytes 9970688 | tf_op jit(solution)/shard_map/dot_general | solution.py:19
  247.3 6.6 convolution_convert_fusion
  254.0 53.6 %reduce-scatter.5.cloned.1.call-done = bf16[256,3072]{1,0:T(8,128)(2,1)} async-done(((bf16[1024,3072]{1,0:T(8,128)(2,1)}), bf16[256,3072]{1,0:T(8,128)(2,1)}) %reduce-scatter.5.cloned.1.call-update) | async-done | bytes 1572880 | tf_op jit(solution)/shard_map/reduce_scatter | solution.py:231
  307.6 74.0 %reduce-scatter.9.cloned.1.call-done = bf16[256,4096]{1,0:T(8,128)(2,1)} async-done(((bf16[1024,4096]{1,0:T(8,128)(2,1)}), bf16[256,4096]{1,0:T(8,128)(2,1)}) %reduce-scatter.9.cloned.1.call-update) | async-done | bytes 2097168 | tf_op jit(solution)/shard_map/reduce_scatter | solution.py:207
  381.6 74.0 %reduce-scatter.11.cloned.1.call-done = bf16[1024,1024]{1,0:T(8,128)(2,1)} async-done(((bf16[4096,1024]{1,0:T(8,128)(2,1)}), bf16[1024,1024]{1,0:T(8,128)(2,1)}) %reduce-scatter.11.cloned.1.call-update) | async-done | bytes 2097168 | tf_op jit(solution)/shard_map/reduce_scatter | solution.py:197
  456.3 5.1 all-gather.7
  464.4 6.9 fusion.37
  471.3 11.3 %all-reduce.11 = (bf16[1024]{0:T(1024)(128)(2,1)S(1)}, bf16[1024]{0:T(1024)(128)(2,1)S(1)}, bf16[1024]{0:T(1024)(128)(2,1)S(1)}, bf16[1024]{0:T(1024)(128)(2,1)S...) all-reduce(bf16[1024]{0:T(1024)(128)(2,1)S(1)} %get-tuple-element.1, ...), channel_id=2, replica_groups=mesh['replica'=8,'shard'=4] {'shard'}, use_global_device_ids=true, to_apply=%region_13.14.clone | all-reduce | flops 12288 | bytes 49152
  483.2 23.3 %all-reduce.9 = (bf16[256]{0:T(256)(128)(2,1)S(1)}, bf16[256]{0:T(256)(128)(2,1)S(1)}, bf16[256]{0:T(256)(128)(2,1)S(1)}, bf16[256]{0:T(256)(128)(2,1)S(1)}, bf1...) all-reduce(bf16[256]{0:T(256)(128)(2,1)S(1)} %dynamic-slice.1, ...), channel_id=1, replica_groups=mesh['replica'=8,'shard'=4] {'replica'}, use_global_device_ids=true, to_apply=%region_14.15 | all-reduce | flops 3072 | bytes 12288 | tf_op jit(solution)/shard_map/psum | solution.py:294
  513.6 5.6 fusion.17
  519.2 152.1 %all-reduce.14.cloned.1.call-done = (bf16[256,3072]{1,0:T(8,128)(2,1)}, bf16[256,1024]{1,0:T(8,128)(2,1)}, bf16[256,4096]{1,0:T(8,128)(2,1)}, bf16[1024,1024]{1,0:T(8,128)(2,1)}) async-done(((bf16[256,3072]{1,0:T(8,128)(2,1)}, bf16[256,1024]{1,0:T(8,128)(2,1)}, bf16[256,4096]{1,0:T(8,128)(2,1)}, bf16[1024,1024]{1,0:T(8,128)(2,1)}), (bf16[256,3072]{1,0:T(8,128)(2,1)}, bf16[256,1024]{1,0:T(8,128)(2,1)}, ...) | async-done | bytes 6291472 | tf_op jit(solution)/shard_map/psum | solution.py:296
  (149 shorter events, 65.9 us)
Async XLA Ops:
  7.2 51.6 %all-gather.13.cloned.1.call-start = ((), (), s32[]{:S(2)}) async-start(), calls=%async_computation.4 | async-start | bytes 7864320 | tf_op jit(solution)/shard_map/all_gather | solution.py:157
  7.9 75.1 %all-gather.15.cloned.1.call-start = ((), (), s32[]{:S(2)}) async-start(), calls=%async_computation.5 | async-start | bytes 2621440 | tf_op jit(solution)/shard_map/all_gather | solution.py:160
  8.7 7.5 %copy-start.17 = (bf16[256]{0:T(256)(128)(2,1)S(1)}, bf16[256]{0:T(256)(128)(2,1)}, u32[]{:S(2)}) copy-start(bf16[256]{0:T(256)(128)(2,1)} %param.20) | copy-start | bytes 1540
  8.7 12.9 %copy-start.18 = (bf16[256]{0:T(256)(128)(2,1)S(1)}, bf16[256]{0:T(256)(128)(2,1)}, u32[]{:S(2)}) copy-start(bf16[256]{0:T(256)(128)(2,1)} %param.19) | copy-start | bytes 1540
  8.7 18.1 %copy-start.19 = (bf16[256]{0:T(256)(128)(2,1)S(1)}, bf16[256]{0:T(256)(128)(2,1)}, u32[]{:S(2)}) copy-start(bf16[256]{0:T(256)(128)(2,1)} %param.22) | copy-start | bytes 1540
  8.7 23.3 %copy-start.20 = (bf16[256]{0:T(256)(128)(2,1)S(1)}, bf16[256]{0:T(256)(128)(2,1)}, u32[]{:S(2)}) copy-start(bf16[256]{0:T(256)(128)(2,1)} %param.23) | copy-start | bytes 1540
  8.7 28.5 %copy-start.15 = (bf16[1024]{0:T(1024)(128)(2,1)S(1)}, bf16[1024]{0:T(1024)(128)(2,1)}, u32[]{:S(2)}) copy-start(bf16[1024]{0:T(1024)(128)(2,1)} %param.29) | copy-start | bytes 6148
  8.7 33.9 %copy-start.21 = (bf16[256]{0:T(256)(128)(2,1)S(1)}, bf16[256]{0:T(256)(128)(2,1)}, u32[]{:S(2)}) copy-start(bf16[256]{0:T(256)(128)(2,1)} %param.27) | copy-start | bytes 1540
  8.7 39.1 %copy-start.22 = (bf16[256]{0:T(256)(128)(2,1)S(1)}, bf16[256]{0:T(256)(128)(2,1)}, u32[]{:S(2)}) copy-start(bf16[256]{0:T(256)(128)(2,1)} %param.26) | copy-start | bytes 1540
  8.7 44.3 %copy-start.23 = (s32[1,4]{1,0:T(1,128)S(1)}, s32[1,4]{1,0:T(1,128)}, u32[]{:S(2)}) copy-start(s32[1,4]{1,0:T(1,128)} %param.18) | copy-start | bytes 52
  8.8 44.6 %copy-start.1 = (bf16[128,1024]{1,0:T(8,128)(2,1)S(1)}, bf16[128,1024]{1,0:T(8,128)(2,1)}, u32[]{:S(2)}) copy-start(bf16[128,1024]{1,0:T(8,128)(2,1)} %param.16) | copy-start | bytes 786436
  8.8 134.1 %all-gather.17.cloned.1.call-start = ((), (), s32[]{:S(2)}) async-start(), calls=%async_computation.6 | async-start | bytes 10485760 | tf_op jit(solution)/shard_map/all_gather | solution.py:164
  9.5 193.0 %all-gather.19.cloned.1.call-start = ((), (), s32[]{:S(2)}) async-start(), calls=%async_computation.7 | async-start | bytes 10485760 | tf_op jit(solution)/shard_map/all_gather | solution.py:166
  10.1 243.9 %reduce-scatter.7.cloned.1.call-start = ((), (), s32[]{:S(2)}) async-start(), calls=%async_computation.9 | async-start | bytes 2621440 | tf_op jit(solution)/shard_map/reduce_scatter | solution.py:218
  63.2 21.9 %copy-start.11 = (bf16[128,1024]{0,1:T(8,128)(2,1)}, bf16[128,1024]{0,1:T(8,128)(2,1)S(1)}, u32[]{:S(2)}) copy-start(bf16[128,1024]{0,1:T(8,128)(2,1)S(1)} %copy.60) | copy-start | bytes 786436
  63.4 21.7 %copy-start.9 = (bf16[128,1024]{0,1:T(8,128)(2,1)}, bf16[128,1024]{0,1:T(8,128)(2,1)S(1)}, u32[]{:S(2)}) copy-start(bf16[128,1024]{0,1:T(8,128)(2,1)S(1)} %copy.61) | copy-start | bytes 786436
  63.8 19.2 %copy-start.8 = (f32[16,128,128]{1,2,0:T(8,128)}, f32[16,128,128]{1,2,0:T(8,128)S(1)}, u32[]{:S(2)}) copy-start(f32[16,128,128]{1,2,0:T(8,128)S(1)} %convolution_multiply_fusion.1) | copy-start | bytes 3145732
  64.3 78.6 %copy-start.12 = (bf16[16,64,128]{2,1,0:T(8,128)(2,1)}, bf16[16,64,128]{2,1,0:T(8,128)(2,1)S(1)}, u32[]{:S(2)}) copy-start(bf16[16,64,128]{2,1,0:T(8,128)(2,1)S(1)} %convolution_convert_fusion.6) | copy-start | bytes 786436
  142.8 59.7 %copy-start.4 = (bf16[128,1024]{1,0:T(8,128)(2,1)S(1)}, bf16[128,1024]{1,0:T(8,128)(2,1)}, u32[]{:S(2)}) copy-start(bf16[128,1024]{1,0:T(8,128)(2,1)} %param.17) | copy-start | bytes 786436
  202.5 7.1 %copy-start = (bf16[1024,4096]{1,0:T(8,128)(2,1)S(1)}, bf16[1024,4096]{1,0:T(8,128)(2,1)}, u32[]{:S(2)}) copy-start(bf16[1024,4096]{1,0:T(8,128)(2,1)} %all-gather.17.cloned.1.call-done) | copy-start | bytes 25165828
  215.0 92.6 %reduce-scatter.5.cloned.1.call-start = ((), (), s32[]{:S(2)}) async-start(), calls=%async_computation.8 | async-start | bytes 7864320 | tf_op jit(solution)/shard_map/reduce_scatter | solution.py:231
  240.3 141.3 %reduce-scatter.9.cloned.1.call-start = ((), (), s32[]{:S(2)}) async-start(), calls=%async_computation.10 | async-start | bytes 10485760 | tf_op jit(solution)/shard_map/reduce_scatter | solution.py:207
  247.3 208.4 %reduce-scatter.11.cloned.1.call-start = ((), (), s32[]{:S(2)}) async-start(), calls=%async_computation.11 | async-start | bytes 10485760 | tf_op jit(solution)/shard_map/reduce_scatter | solution.py:197
  253.9 417.3 %all-reduce.14.cloned.1.call-start = ((), (), s32[]{:S(2)}) async-start(), calls=%async_computation.12 | async-start | bytes 12582912 | tf_op jit(solution)/shard_map/psum | solution.py:296
  (11 other events, 33.3 us)
Sparse Core Ops, SparseCore 0:
  9.6 49.2 all-gather.12
  60.4 22.5 all-gather.14
  84.5 58.2 all-gather.16
  144.2 58.2 all-gather.18
  215.1 31.1 reduce-scatter.6
  248.7 58.8 reduce-scatter.4
  310.2 71.3 reduce-scatter.8
  384.2 71.4 reduce-scatter.10
  460.1 211.1 all-reduce.13
where the time goes:
time: 688 us; the launch traced here: 687 us
  waiting for transfers between devices  493 us (72%)
  blocking collectives  82.4 us (12%)
  matrix products  69.8 us (10%)
  other arithmetic  22.1 us (3%)
  between operations  15.6 us (2%)
    psum x1, waiting for transfers between devices, local(): lax.psum(qkv_owned, 'replica').astype(jnp.float32)  152 us
    reduce_scatter x1, waiting for transfers between devices, local(): lax.psum_scatter(column_term(activated, out_grad).astype(jnp.bfloat16), '...  74 us
    reduce_scatter x1, waiting for transfers between devices, local(): lax.psum_scatter(column_term(second_in, pre_round).astype(jnp.bfloat16),...  74 us
    all_gather x1, waiting for transfers between devices, local(): lax.all_gather(up_weight, 'shard', axis=0, tiled=True)  57.5 us
    all_gather x1, waiting for transfers between devices, local(): lax.all_gather(down_weight, 'shard', axis=0, tiled=True)  54.9 us
    reduce_scatter x1, waiting for transfers between devices, local(): lax.psum_scatter(column_term(first_in, qkv_grad).astype(jnp.bfloat16), 's...  53.6 us
    psum x1, blocking collectives, local(): lax.psum(gain1_own.astype(jnp.bfloat16), 'replica').astype(jnp.float32)  23.3 us
    dot_general x4, matrix products, left_product(): lax.dot_general(left, right, (((0,), (0,)), ((), ())), preferred_element_...  21.3 us
  transfers between devices with their start and end apart: 9, of which 8 were waited for; matrix products, arithmetic and copies ran while one was open for 11% of the time, Pallas kernels for 0%

commit v1 on v0

--- a/solution.py
+++ b/solution.py
@@ -9,6 +9,28 @@
 EPSILON = 1e-05
 TANH_SCALE = math.sqrt(2.0 / math.pi)
 CUBIC = 0.044715
+
+
+def joined_along(blocks, dim):
+    blocks = jnp.moveaxis(blocks, 0, dim)
+    dims = blocks.shape
+    return blocks.reshape(*dims[:dim], dims[dim] * dims[dim + 1], *dims[dim + 2 :])
+
+
+def collected_by_bits(x, axis):
+    size = lax.axis_size(axis)
+    blocks = x[None]
+    for level in range(size.bit_length() - 1):
+        bit = 1 << level
+        partner_block = lax.ppermute(blocks, axis, [(i, i ^ bit) for i in range(size)])
+        both = jnp.stack([blocks, partner_block])
+        upper = lax.axis_index(axis) >> level & 1
+        blocks = jnp.where(upper == 0, both, both[::-1]).reshape(-1, *x.shape)
+    return blocks
+
+
+def gather_by_bits(array, axis, dim):
+    return joined_along(collected_by_bits(array, axis), dim)
 
 
 def product(left, right):
@@ -161,7 +183,7 @@
         lax.all_gather(out_bias, "shard", axis=0, tiled=True),
         lax.all_gather(norm2_gain, "shard", axis=0, tiled=True),
         lax.all_gather(norm2_bias, "shard", axis=0, tiled=True),
-        lax.all_gather(up_weight, "shard", axis=0, tiled=True),
+        gather_by_bits(up_weight, "shard", 0),
         lax.all_gather(up_bias, "shard", axis=0, tiled=True),
         lax.all_gather(down_weight, "shard", axis=0, tiled=True),
         lax.all_gather(down_bias, "shard", axis=0, tiled=True),

time: 688 us -> 740 us (1.076)
  blocking collectives: 82.4 us -> 231 us
  waiting for transfers between devices: 493 us -> 360 us
  other arithmetic: 22.1 us -> 50.2 us
    all_gather x1, blocking collectives: 6.02 us -> 155 us  [local(): lax.all_gather(out_bias, 'shard', axis=0, tiled=True)]
    all_gather x1 -> x0, waiting for transfers between devices: 57.5 us -> none  [local(): lax.all_gather(up_weight, 'shard', axis=0, tiled=True)]
    all_gather x1, waiting for transfers between devices: 54.9 us -> 0.02 us  [local(): lax.all_gather(down_weight, 'shard', axis=0, tiled=True)]
    all_gather x1, waiting for transfers between devices: 18.7 us -> 0.02 us  [local(): lax.all_gather(out_weight, 'shard', axis=0, tiled=True)]
    another operation x0 -> x3, other arithmetic: none -> 14.6 us  [collected_by_bits(): both = jnp.stack([blocks, partner_block])]
    select_n x0 -> x1, other arithmetic: none -> 13.5 us  [collected_by_bits(): blocks = jnp.where(upper == 0, both, both[::-1]).reshape(-1, *x.shape)]
  transfers between devices with their start and end apart: 9 -> 10, of which waited for: 8 -> 5; matrix products, arithmetic and copies ran while one was open for 11% -> 14% of each run, Pallas kernels for 0% -> 0%
where the time goes in v1:
time: 740 us; the launch traced here: 739 us
  waiting for transfers between devices  360 us (49%)
  blocking collectives  231 us (31%)
  matrix products  73.7 us (10%)
  other arithmetic  50.2 us (7%)
  between operations  15.9 us (2%)
    all_gather x1, blocking collectives, local(): lax.all_gather(out_bias, 'shard', axis=0, tiled=True)  155 us
    psum x1, waiting for transfers between devices, local(): lax.psum(qkv_owned, 'replica').astype(jnp.float32)  152 us
    reduce_scatter x1, waiting for transfers between devices, local(): lax.psum_scatter(column_term(second_in, pre_round).astype(jnp.bfloat16),...  74 us
    reduce_scatter x1, waiting for transfers between devices, local(): lax.psum_scatter(column_term(activated, out_grad).astype(jnp.bfloat16), '...  73.9 us
    reduce_scatter x1, waiting for transfers between devices, local(): lax.psum_scatter(column_term(first_in, qkv_grad).astype(jnp.bfloat16), 's...  53.7 us
    psum x1, blocking collectives, local(): lax.psum(gain1_own.astype(jnp.bfloat16), 'replica').astype(jnp.float32)  23 us
    dot_general x4, matrix products, right_product(): lax.dot_general(left, right, (((1,), (1,)), ((), ())), preferred_element_...  22.3 us
    dot_general x4, matrix products, left_product(): lax.dot_general(left, right, (((0,), (0,)), ((), ())), preferred_element_...  21.3 us
  transfers between devices with their start and end apart: 10, of which 5 were waited for; matrix products, arithmetic and copies ran while one was open for 14% of the time, Pallas kernels for 0%

profile of v1, /device:TPU:0, one launch (start us, length us, event | category | flops | bytes accessed | tf_op | source)
XLA Modules:
  0.0 739.1 jit_solution(15148538930673795989)
XLA Ops:
  16.0 5.1 fusion.3
  24.3 154.9 %all-gather.4 = bf16[4,1,256]{2,1,0:T(2,128)(2,1)S(1)} all-gather(bf16[1,1,256]{2,1,0:T(2,128)(2,1)S(1)} %reshape.295), channel_id=1, replica_groups=mesh['replica'=8,'shard'=4] {'shard'}, dimensions={0}, use_global_device_ids=true | all-gather | bytes 2560 | tf_op jit(solution)/shard_map/all_gather | solution.py:183
  179.2 5.2 all-gather.1
  184.5 5.2 all-gather
  189.7 5.2 all-gather.3
  194.9 5.2 all-gather.2
  200.3 5.2 all_gather.45
  205.5 5.1 all-gather.6
  210.6 5.2 all-gather.5
  216.4 7.5 %pad_maximum_fusion = bf16[2,2,256,4096]{3,2,1,0:T(8,128)(2,1)} fusion(bf16[1,2,256,4096]{3,2,1,0:T(8,128)(2,1)} %bitcast.19, bf16[1,2,256,4096]{3,2,1,0:T(8,128)(2,1)} %get-tuple-element.47), kind=kLoop, calls=%fused_computation.3 | loop fusion | flops 4194304 | bytes 16777216 | tf_op jit(solution)/shard_map/stack | solution.py:26
  223.8 13.5 %reverse_select_fusion = bf16[2,2,256,4096]{3,2,1,0:T(8,128)(2,1)} fusion(bf16[2,2,256,4096]{3,2,1,0:T(8,128)(2,1)} %pad_maximum_fusion, pred[]{:T(512)S(6)} %eq.28), kind=kLoop, calls=%fused_computation.2 | loop fusion | flops 4194304 | bytes 16777216 | tf_op jit(solution)/shard_map/jit(_where)/select_n | solution.py:28
  250.1 6.9 fusion.76
  257.1 7.0 multiply_reduce_fusion.1
  285.7 5.8 convolution_convert_fusion.2
  291.5 6.6 convolution_convert_fusion
  298.4 6.9 convolution_convert_fusion.1
  305.4 53.7 %reduce-scatter.5.cloned.1.call-done = bf16[256,3072]{1,0:T(8,128)(2,1)} async-done(((bf16[1024,3072]{1,0:T(8,128)(2,1)}), bf16[256,3072]{1,0:T(8,128)(2,1)}) %reduce-scatter.5.cloned.1.call-update) | async-done | bytes 1572880 | tf_op jit(solution)/shard_map/reduce_scatter | solution.py:253
  359.1 73.9 %reduce-scatter.11.cloned.1.call-done = bf16[1024,1024]{1,0:T(8,128)(2,1)} async-done(((bf16[4096,1024]{1,0:T(8,128)(2,1)}), bf16[1024,1024]{1,0:T(8,128)(2,1)}) %reduce-scatter.11.cloned.1.call-update) | async-done | bytes 2097168 | tf_op jit(solution)/shard_map/reduce_scatter | solution.py:219
  432.9 74.0 %reduce-scatter.9.cloned.1.call-done = bf16[256,4096]{1,0:T(8,128)(2,1)} async-done(((bf16[1024,4096]{1,0:T(8,128)(2,1)}), bf16[256,4096]{1,0:T(8,128)(2,1)}) %reduce-scatter.9.cloned.1.call-update) | async-done | bytes 2097168 | tf_op jit(solution)/shard_map/reduce_scatter | solution.py:229
  515.7 6.8 fusion.39
  522.6 11.3 %all-reduce.11 = (bf16[1024]{0:T(1024)(128)(2,1)S(1)}, bf16[1024]{0:T(1024)(128)(2,1)S(1)}, bf16[1024]{0:T(1024)(128)(2,1)S(1)}, bf16[1024]{0:T(1024)(128)(2,1)S...) all-reduce(bf16[1024]{0:T(1024)(128)(2,1)S(1)} %get-tuple-element.1, ...), channel_id=2, replica_groups=mesh['replica'=8,'shard'=4] {'shard'}, use_global_device_ids=true, to_apply=%region_13.14.clone | all-reduce | flops 12288 | bytes 49152
  534.5 23.0 %all-reduce.9 = (bf16[256]{0:T(256)(128)(2,1)S(1)}, bf16[256]{0:T(256)(128)(2,1)S(1)}, bf16[256]{0:T(256)(128)(2,1)S(1)}, bf16[256]{0:T(256)(128)(2,1)S(1)}, bf1...) all-reduce(bf16[256]{0:T(256)(128)(2,1)S(1)} %dynamic-slice.1, ...), channel_id=1, replica_groups=mesh['replica'=8,'shard'=4] {'replica'}, use_global_device_ids=true, to_apply=%region_14.15 | all-reduce | flops 3072 | bytes 12288 | tf_op jit(solution)/shard_map/psum | solution.py:316
  564.6 5.6 fusion.19
  570.2 152.3 %all-reduce.14.cloned.1.call-done = (bf16[256,3072]{1,0:T(8,128)(2,1)}, bf16[256,1024]{1,0:T(8,128)(2,1)}, bf16[256,4096]{1,0:T(8,128)(2,1)}, bf16[1024,1024]{1,0:T(8,128)(2,1)}) async-done(((bf16[256,3072]{1,0:T(8,128)(2,1)}, bf16[256,1024]{1,0:T(8,128)(2,1)}, bf16[256,4096]{1,0:T(8,128)(2,1)}, bf16[1024,1024]{1,0:T(8,128)(2,1)}), (bf16[256,3072]{1,0:T(8,128)(2,1)}, bf16[256,1024]{1,0:T(8,128)(2,1)}, ...) | async-done | bytes 6291472 | tf_op jit(solution)/shard_map/psum | solution.py:318
  (154 shorter events, 72.1 us)
Async XLA Ops:
  7.2 230.2 %all-gather.12.cloned.1.call-start = ((), (), s32[]{:S(2)}) async-start(), calls=%async_computation.4 | async-start | bytes 7864320 | tf_op jit(solution)/shard_map/all_gather | solution.py:179
  7.9 234.9 %all-gather.14.cloned.1.call-start = ((), (), s32[]{:S(2)}) async-start(), calls=%async_computation.5 | async-start | bytes 2621440 | tf_op jit(solution)/shard_map/all_gather | solution.py:182
  8.7 241.4 %all-gather.16.cloned.1.call-start = ((), (), s32[]{:S(2)}) async-start(), calls=%async_computation.6 | async-start | bytes 10485760 | tf_op jit(solution)/shard_map/all_gather | solution.py:188
  9.4 296.0 %reduce-scatter.7.cloned.1.call-start = ((), (), s32[]{:S(2)}) async-start(), calls=%async_computation.8 | async-start | bytes 2621440 | tf_op jit(solution)/shard_map/reduce_scatter | solution.py:240
  9.5 4.5 collective-permute-start
  15.9 8.4 %copy-start.16 = (bf16[256]{0:T(256)(128)(2,1)S(1)}, bf16[256]{0:T(256)(128)(2,1)}, u32[]{:S(2)}) copy-start(bf16[256]{0:T(256)(128)(2,1)} %param.25) | copy-start | bytes 1540
  15.9 163.3 %copy-start.17 = (bf16[256]{0:T(256)(128)(2,1)S(1)}, bf16[256]{0:T(256)(128)(2,1)}, u32[]{:S(2)}) copy-start(bf16[256]{0:T(256)(128)(2,1)} %param.20) | copy-start | bytes 1540
  15.9 168.5 %copy-start.18 = (bf16[256]{0:T(256)(128)(2,1)S(1)}, bf16[256]{0:T(256)(128)(2,1)}, u32[]{:S(2)}) copy-start(bf16[256]{0:T(256)(128)(2,1)} %param.19) | copy-start | bytes 1540
  16.0 173.7 %copy-start.19 = (bf16[256]{0:T(256)(128)(2,1)S(1)}, bf16[256]{0:T(256)(128)(2,1)}, u32[]{:S(2)}) copy-start(bf16[256]{0:T(256)(128)(2,1)} %param.22) | copy-start | bytes 1540
  16.0 178.9 %copy-start.20 = (bf16[256]{0:T(256)(128)(2,1)S(1)}, bf16[256]{0:T(256)(128)(2,1)}, u32[]{:S(2)}) copy-start(bf16[256]{0:T(256)(128)(2,1)} %param.23) | copy-start | bytes 1540
  16.0 184.2 %copy-start.21 = (s32[1,4]{1,0:T(1,128)S(1)}, s32[1,4]{1,0:T(1,128)}, u32[]{:S(2)}) copy-start(s32[1,4]{1,0:T(1,128)} %param.18) | copy-start | bytes 52
  16.0 184.3 %copy-start.15 = (bf16[1024]{0:T(1024)(128)(2,1)S(1)}, bf16[1024]{0:T(1024)(128)(2,1)}, u32[]{:S(2)}) copy-start(bf16[1024]{0:T(1024)(128)(2,1)} %param.29) | copy-start | bytes 6148
  16.0 189.5 %copy-start.22 = (bf16[256]{0:T(256)(128)(2,1)S(1)}, bf16[256]{0:T(256)(128)(2,1)}, u32[]{:S(2)}) copy-start(bf16[256]{0:T(256)(128)(2,1)} %param.27) | copy-start | bytes 1540
  16.0 194.6 %copy-start.23 = (bf16[256]{0:T(256)(128)(2,1)S(1)}, bf16[256]{0:T(256)(128)(2,1)}, u32[]{:S(2)}) copy-start(bf16[256]{0:T(256)(128)(2,1)} %param.26) | copy-start | bytes 1540
  16.0 199.9 %copy-start = (bf16[128,1024]{1,0:T(8,128)(2,1)S(1)}, bf16[128,1024]{1,0:T(8,128)(2,1)}, u32[]{:S(2)}) copy-start(bf16[128,1024]{1,0:T(8,128)(2,1)} %param.16) | copy-start | bytes 786436
  21.2 195.2 %collective-permute-start.1 = (bf16[2,256,4096]{2,1,0:T(8,128)(2,1)}, bf16[2,256,4096]{2,1,0:T(8,128)(2,1)}, u32[]{:S(2)}, u32[]{:S(2)}) collective-permute-start(bf16[2,256,4096]{2,1,0:T(8,128)(2,1)} %get-tuple-element.48), channel_id=1, source_target_pairs={{0,2},{1,3},{2,0},{3,1},{4,6},{5,7},{6,4},{7,5},{8,10},{9,11},{10,... | collective-permute-start | bytes 12582920 | tf_op jit(solution)/shard_map/ppermute | solution.py:25
  257.0 7.1 copy-start.2
  257.0 7.1 copy-start.4
  257.1 7.3 copy-start.13
  266.4 92.6 %reduce-scatter.5.cloned.1.call-start = ((), (), s32[]{:S(2)}) async-start(), calls=%async_computation.7 | async-start | bytes 7864320 | tf_op jit(solution)/shard_map/reduce_scatter | solution.py:253
  291.5 141.5 %reduce-scatter.11.cloned.1.call-start = ((), (), s32[]{:S(2)}) async-start(), calls=%async_computation.10 | async-start | bytes 10485760 | tf_op jit(solution)/shard_map/reduce_scatter | solution.py:219
  298.1 208.8 %reduce-scatter.9.cloned.1.call-start = ((), (), s32[]{:S(2)}) async-start(), calls=%async_computation.9 | async-start | bytes 10485760 | tf_op jit(solution)/shard_map/reduce_scatter | solution.py:229
  305.3 417.2 %all-reduce.14.cloned.1.call-start = ((), (), s32[]{:S(2)}) async-start(), calls=%async_computation.11 | async-start | bytes 12582912 | tf_op jit(solution)/shard_map/psum | solution.py:318
  506.9 6.7 copy-start.25
  (12 other events, 32.2 us)
Sparse Core Ops, SparseCore 0:
  9.6 80.5 all-gather.11
  91.7 33.0 all-gather.13
  126.4 78.4 all-gather.15
  266.5 31.2 reduce-scatter.6
  300.2 58.8 reduce-scatter.4
  361.5 71.3 reduce-scatter.10
  435.5 71.3 reduce-scatter.8
  511.4 211.1 all-reduce.13
